TPU v7x, 32 devices: a whole 2x2x4 slice. The times are simulated.
32 devices in a mesh: groups: 2 (over y), section: 2 (over core), row: 2 (over x), col: 4 (over z).
Axes of the slice: x: 2, y: 2, z: 4, core: 2. Of those that a mesh axis runs over, the one named last changes fastest.
Arguments:
- hidden: bfloat16 [2, 2, 3072, 8192], P('section', None, ('groups', 'col'), 'row'), parts along dimension 2, may hold values from -400 to 400
- upstream: bfloat16 [2, 3072, 8192], P(None, ('groups', 'col'), 'row'), parts along dimension 1, may hold values from -8 to 8
- weights: bfloat16 [2, 8192, 8192], P('section', 'row', 'col'), may hold values from -0.0625 to 0.0625
- norm_gains: bfloat16 [2, 8192], P('section', 'row'), may hold values from 0.5 to 1.5
- steering: bfloat16 [16384], P(('groups', 'row')), parts along dimension 0, may hold values from -18 to 18
- steer_layer: int32 [2, 3072], P(None, ('groups', 'col')), parts along dimension 1, may hold values from 0 to 1
Outputs:
- section_grads: bfloat16 [2, 2, 3072, 8192], P('section', None, ('groups', 'col'), 'row'), parts along dimension 2
- steer_grad: float32 [16384], P(('groups', 'row')), parts along dimension 0
There are 2 independent parts, one for each index of `groups`. A program takes and returns all parts, laid end to end along the dimension named above; an argument that names none is the same for every part. Nothing has to cross between parts.
All inputs are finite; a program needn't handle non-finite values.
Results may differ from a plain program's by a relative error of at most 0.0038.
Values may be sent and summed in bfloat16 or wider, within the bound.
A program may use at most 320 MiB of HBM per device.

v0:
```python
import jax
import jax.numpy as jnp
from jax import lax
from jax.sharding import PartitionSpec as P

D = 8192
ROWS = 1536
MICRO = 2
epsilon = 1e-06


def passed_along(value, axis, steps):
    count = lax.axis_size(axis)
    initial, last = (max(0, -steps), min(count, count - steps))
    return lax.ppermute(value, axis, [(source, source + steps) for source in range(initial, last)])


def local(hidden, upstream, weights, norm_gains, steering, steer_layer):
    sections = lax.axis_size("section")
    section_index = lax.axis_index("section")
    scaling = norm_gains[0].astype(jnp.float32)
    steer_vec = steering.astype(jnp.float32)
    unsteered_all = hidden[0].astype(jnp.float32)
    moved_all = unsteered_all + steer_vec
    row_count = unsteered_all.shape[1]
    feature_count = unsteered_all.shape[2]
    local_weight = weights[0]
    contract = (((1,), (1,)), ((), ()))

    def regroup(full):
        split = full.reshape(row_count, cols, groups, piece)
        return jnp.swapaxes(split, 1, 2).reshape(row_count, cols * groups * piece)

    groups = lax.axis_size("groups")
    cols = lax.axis_size("col")
    piece = local_weight.shape[1] // groups
    own_piece = lax.dynamic_slice_in_dim(local_weight, lax.axis_index("groups") * piece, piece, 1)
    full_weight = lax.all_gather(own_piece, ("groups", "col"), axis=1, tiled=True)
    ticks = MICRO + sections - 1
    received = jnp.zeros((row_count, feature_count), jnp.bfloat16)
    results = jnp.zeros((MICRO, row_count, feature_count), jnp.bfloat16)
    steer_part = jnp.zeros((feature_count,), jnp.float32)
    slots = jnp.arange(MICRO, dtype=jnp.int32)
    for tick_index in range(ticks):
        micro_index = tick_index - (sections - 1 - section_index)
        active = (micro_index >= 0) & (micro_index < MICRO)
        clipped = jnp.clip(micro_index, 0, MICRO - 1)
        if tick_index < MICRO:
            upstream_block = upstream[tick_index]
        else:
            upstream_block = jnp.zeros_like(upstream[0])
        grad_in = jnp.where(section_index == sections - 1, upstream_block, received)
        unsteered = lax.dynamic_index_in_dim(unsteered_all, clipped, 0, keepdims=False)
        moved = lax.dynamic_index_in_dim(moved_all, clipped, 0, keepdims=False)
        layer_rows = lax.dynamic_index_in_dim(steer_layer, clipped, 0, keepdims=False)
        steered = layer_rows == section_index
        steered_col = steered[:, None]
        normal_grad = lax.dot_general(
            regroup(lax.all_gather(grad_in, "row", axis=1, tiled=True)),
            full_weight,
            contract,
            preferred_element_type=jnp.float32,
        )
        grad_float = grad_in.astype(jnp.float32)
        scaled = scaling * normal_grad
        plain_local = jnp.sum(unsteered * unsteered, -1)
        moved_local = jnp.sum(moved * moved, -1)
        scaled_plain = jnp.sum(scaled * unsteered, -1)
        scaled_moved = jnp.sum(scaled * moved, -1)
        plain_sq, moved_sq, curve_plain, curve_moved = lax.psum(
            (plain_local, moved_local, scaled_plain, scaled_moved), "row"
        )
        norm_plain = jnp.sqrt(plain_sq + epsilon)
        norm_moved = jnp.sqrt(moved_sq + epsilon)
        rescale = norm_plain / norm_moved
        square_sum = jnp.where(
            steered, norm_plain * norm_plain * moved_sq / (norm_moved * norm_moved), plain_sq
        )
        root_mean = jnp.sqrt(square_sum / D + epsilon)
        curvature = jnp.where(steered, rescale * curve_moved, curve_plain)
        rescaled = jnp.where(steered_col, moved * rescale[:, None], unsteered)
        factor = curvature / (D * root_mean**3)
        input_grad = grad_float + scaled / root_mean[:, None] - rescaled * factor[:, None]
        direction = moved / norm_moved[:, None]
        radial = lax.psum(jnp.sum(direction * input_grad, -1), "row")
        tangent = rescale[:, None] * (input_grad - direction * radial[:, None])
        below = jnp.where(
            steered_col, tangent + unsteered / norm_plain[:, None] * radial[:, None], input_grad
        )
        passed = jnp.where(active, below, 0.0).astype(jnp.bfloat16)
        results = jnp.where((slots == micro_index)[:, None, None], passed[None], results)
        steer_part = steer_part + jnp.sum(jnp.where(active & steered_col, tangent, 0.0), 0)
        if tick_index + 1 < ticks:
            received = passed_along(passed, "section", -1)
    steer_total = lax.psum(steer_part, ("section", "col"))
    return (results[None], steer_total / (MICRO * ROWS))


def solution(mesh):
    placed = (
        P("section", None, ("groups", "col"), "row"),
        P(None, ("groups", "col"), "row"),
        P("section", "row", "col"),
        P("section", "row"),
        P(("groups", "row")),
        P(None, ("groups", "col")),
    )
    return jax.shard_map(
        local,
        mesh=mesh,
        in_specs=placed,
        out_specs=(P("section", None, ("groups", "col"), "row"), P(("groups", "row"))),
        check_vma=False,
    )
```

profile of v0, /device:TPU:1, one launch (start us, length us, event | category | flops | bytes accessed | tf_op | source)
XLA Modules:
  0.0 1859.2 jit_solution(14400749378231385533)
XLA Ops:
  7.2 0.0 all-gather.11.cloned.1.call-start
  7.2 3.8 slice_select_fusion
  11.0 0.0 all-gather.11.cloned.1.call-update
  11.0 0.0 all-gather.13.cloned.1.call-start
  11.1 7.7 constant_dynamic-slice_fusion
  18.7 0.0 all-gather.7.cloned.1.call-start
  18.8 0.6 copy-done.11
  19.5 10.7 convert_element_type.29
  30.2 0.6 compare_reduce_fusion.2
  30.8 9.0 bitcast_add_fusion
  39.8 53.8 %all-gather.11.cloned.1.call-done = bf16[1,384,8192]{2,1,0:T(8,128)(2,1)} async-done(((bf16[1,384,4096]{2,1,0:T(8,128)(2,1)}), bf16[1,384,8192]{2,1,0:T(8,128)(2,1)}) %all-gather.11.cloned.1.call-update) | async-done | bytes 6291472 | tf_op jit(solution)/shard_map/all_gather | solution.py:59
  93.6 11.2 reshape.112
  104.8 16.4 copy.8
  121.3 1240.8 %all-gather.13.cloned.1.call-done = bf16[1,4096,8192]{2,1,0:T(8,128)(2,1)} async-done(((bf16[1,4096,1024]{2,1,0:T(8,128)(2,1)}), bf16[1,4096,8192]{2,1,0:T(8,128)(2,1)}) %all-gather.13.cloned.1.call-update) | async-done | bytes 67108880 | tf_op jit(solution)/shard_map/all_gather | solution.py:38
  1362.1 36.7 %fusion.10 = (f32[384]{0:T(512)S(1)}, f32[384]{0:T(512)S(1)}, f32[384]{0:T(512)S(1)}, f32[384]{0:T(512)S(1)}, f32[384,4096]{1,0:T(8,128)}) fusion(f32[2,384,4096]{2,1,0:T(8,128)} %bitcast_add_fusion, s32[]{:T(128)S(6)} %min.12, f32[1,2,384,4096]{3,2,1,0:T(8,128)} %convert_element_type.29, bf16[384,8192]{0,1:T(8,128)(2,1)} %bitcast.166, ...), kind=kOutput, calls=%fused_computation.16 | convolution fusion | flops 25783959552 | bytes 92297216 | tf_op jit(solution)/shard_map/dot_general | solution.py:58
  1398.8 3.8 all-reduce.2
  1402.7 11.2 multiply_reduce_fusion.2
  1413.8 3.8 psum.120
  1417.6 8.1 fusion.41
  1425.8 1.7 copy-done.2
  1427.4 5.2 collective-permute-start
  1432.7 4.9 collective-permute-done
  1437.6 3.9 bitcast_select_fusion
  1441.5 0.0 all-gather.9.cloned.1.call-start
  1441.6 81.4 %all-gather.7.cloned.1.call-done = bf16[384,8192]{1,0:T(8,128)(2,1)} async-done(((bf16[384,4096]{1,0:T(8,128)(2,1)}), bf16[384,8192]{1,0:T(8,128)(2,1)}) %all-gather.7.cloned.1.call-update) | async-done | bytes 6291472 | tf_op jit(solution)/shard_map/all_gather | solution.py:59
  1523.0 11.1 reshape.114
  1534.1 16.3 copy.9
  1550.4 36.9 %fusion.21 = (f32[384]{0:T(512)S(1)}, f32[384]{0:T(512)S(1)}, f32[384]{0:T(512)S(1)}, f32[384]{0:T(512)S(1)}, f32[384,4096]{1,0:T(8,128)}) fusion(f32[2,384,4096]{2,1,0:T(8,128)} %bitcast_add_fusion, s32[]{:T(128)S(6)} %min.11, f32[1,2,384,4096]{3,2,1,0:T(8,128)} %convert_element_type.29, bf16[384,8192]{0,1:T(8,128)(2,1)} %bitcast.168, ...), kind=kOutput, calls=%fused_computation.34 | convolution fusion | flops 25783959552 | bytes 92297216 | tf_op jit(solution)/shard_map/dot_general | solution.py:58
  1587.4 3.8 all-reduce.1
  1591.2 10.4 multiply_reduce_fusion.1
  1601.7 3.8 psum.123
  1605.4 8.1 fusion.40
  1613.6 1.6 copy-done.4
  1615.1 5.4 collective-permute-start.1
  1620.6 4.8 collective-permute-done.1
  1625.4 1.8 broadcast_select_fusion
  1627.4 80.2 %all-gather.9.cloned.1.call-done = bf16[384,8192]{1,0:T(8,128)(2,1)} async-done(((bf16[384,4096]{1,0:T(8,128)(2,1)}), bf16[384,8192]{1,0:T(8,128)(2,1)}) %all-gather.9.cloned.1.call-update) | async-done | bytes 6291472 | tf_op jit(solution)/shard_map/all_gather | solution.py:59
  1707.5 11.1 reshape.116
  1718.6 16.2 copy.10
  1734.9 36.7 %fusion.32 = (f32[384]{0:T(512)S(1)}, f32[384]{0:T(512)S(1)}, f32[384]{0:T(512)S(1)}, f32[384]{0:T(512)S(1)}, f32[384,4096]{1,0:T(8,128)}) fusion(f32[2,384,4096]{2,1,0:T(8,128)} %bitcast_add_fusion, s32[]{:T(128)S(6)} %min.10, f32[1,2,384,4096]{3,2,1,0:T(8,128)} %convert_element_type.29, bf16[384,8192]{0,1:T(8,128)(2,1)} %bitcast.167, ...), kind=kOutput, calls=%fused_computation.52 | convolution fusion | flops 25783959552 | bytes 92297216 | tf_op jit(solution)/shard_map/dot_general | solution.py:58
  1771.6 3.8 all-reduce
  1775.5 10.5 multiply_reduce_fusion
  1785.9 3.8 psum.126
  1789.7 9.4 fusion.39
  1799.1 14.4 select_reduce_fusion.1
  1813.6 31.8 %psum.127 = f32[4096]{0:T(1024)S(1)} all-reduce(f32[4096]{0:T(1024)S(1)} %add_add_fusion), channel_id=1, replica_groups=mesh['groups'=2,'section'=2,'row'=2,'col'=4] {'section','col'}, use_global_device_ids=true, to_apply=%region_33.34 | all-reduce | flops 4096 | bytes 32768 | tf_op jit(solution)/shard_map/psum | solution.py:95
  1845.3 0.6 broadcast_multiply_fusion
  1846.0 6.7 select_select_fusion
  (41 shorter events, 0.2 us)
Async XLA Ops:
  7.2 86.4 %all-gather.11.cloned.1.call-start = ((), (), s32[]{:S(2)}) async-start(), calls=%async_computation.2 | async-start | bytes 9437184 | tf_op jit(solution)/shard_map/all_gather | solution.py:59
  11.0 1351.1 %all-gather.13.cloned.1.call-start = ((), (), s32[]{:S(2)}) async-start(), calls=%async_computation.3 | async-start | bytes 75497472 | tf_op jit(solution)/shard_map/all_gather | solution.py:38
  18.7 0.7 copy-start.11
  18.7 0.7 copy-start.13
  18.7 1504.2 %all-gather.7.cloned.1.call-start = ((), (), s32[]{:S(2)}) async-start(), calls=%async_computation | async-start | bytes 9437184 | tf_op jit(solution)/shard_map/all_gather | solution.py:59
  19.5 10.7 copy-start.14
  1402.6 15.0 copy-start.5
  1402.7 15.0 copy-start.7
  1417.6 8.1 copy-start.9
  1425.8 1.7 copy-start.2
  1427.4 10.1 collective-permute-start
  1441.5 266.0 %all-gather.9.cloned.1.call-start = ((), (), s32[]{:S(2)}) async-start(), calls=%async_computation.1 | async-start | bytes 9437184 | tf_op jit(solution)/shard_map/all_gather | solution.py:59
  1550.4 40.8 %copy-start.1 = (bf16[384,4096]{1,0:T(8,128)(2,1)S(1)}, bf16[384,4096]{1,0:T(8,128)(2,1)}, u32[]{:S(2)}) copy-start(bf16[384,4096]{1,0:T(8,128)(2,1)} %bitcast_select_fusion) | copy-start | bytes 9437188
  1613.5 1.6 copy-start.4
  1615.1 12.2 copy-start.12
  1615.1 10.3 collective-permute-start.1
  1789.7 9.4 copy-start
  1789.7 9.4 copy-start.6
  1789.7 9.4 copy-start.8
  1789.7 9.4 copy-start.10
  1799.1 46.9 %copy-start.3 = (bf16[384,4096]{1,0:T(8,128)(2,1)S(1)}, bf16[384,4096]{1,0:T(8,128)(2,1)}, u32[]{:S(2)}) copy-start(bf16[384,4096]{1,0:T(8,128)(2,1)} %copy-done.2) | copy-start | bytes 9437188
Sparse Core Ops, SparseCore 0:
  11.1 82.4 all-gather.10
  95.1 1266.8 all-gather.12
  1441.6 81.2 all-gather.6
  1627.4 80.0 all-gather.8
where the time goes:
time: 1860 us
  waiting for transfers between devices  1470 us (79%)
  matrix products  110 us (6%)
  other arithmetic  109 us (6%)
  local copies, waits for them, and re-layouts  94.1 us (5%)
  blocking collectives  54.5 us (3%)
    all_gather x1, waiting for transfers between devices, local(): lax.all_gather(own_piece, ('groups', 'col'), axis=1, tiled=True)  1240 us
    all_gather x3, waiting for transfers between devices, local(): lax.all_gather(grad_in, 'row', axis=1, tiled=True)  215 us
    dot_general x3, matrix products, local(): lax.dot_general(regroup(lax.all_gather(grad_in, 'row', axis=1, tiled=True...  110 us
    reshape x6, local copies, waits for them, and re-layouts, regroup(): split = full.reshape(row_count, cols, groups, piece)  82.5 us
  transfers between devices with their start and end apart: 6, of which 6 were waited for; matrix products, arithmetic and copies ran while one was open for 3% of the time, Pallas kernels for 0%

commit v1 on v0

--- a/solution.py
+++ b/solution.py
@@ -7,6 +7,23 @@
 ROWS = 1536
 MICRO = 2
 epsilon = 1e-06
+
+
+def track_cubes_now(my_data):
+    upper, piece_now, outcome_arr = (lax.axis_size("row"), lax.axis_index("row"), my_data.shape[1])
+    next_value, arr_next = (my_data, 1)
+    while arr_next < upper:
+        next_value = jnp.concatenate(
+            [
+                next_value,
+                lax.ppermute(
+                    next_value, "row", tuple(((m, (m - arr_next) % upper) for m in range(upper)))
+                ),
+            ],
+            1,
+        )
+        arr_next = 2 * arr_next
+    return jnp.roll(next_value, piece_now * outcome_arr, axis=1)
 
 
 def passed_along(value, axis, steps):
@@ -56,7 +73,7 @@
         steered = layer_rows == section_index
         steered_col = steered[:, None]
         normal_grad = lax.dot_general(
-            regroup(lax.all_gather(grad_in, "row", axis=1, tiled=True)),
+            regroup(track_cubes_now(grad_in)),
             full_weight,
             contract,
             preferred_element_type=jnp.float32,

time: 1860 us -> 1760 us (0.946)
  waiting for transfers between devices: 1470 us -> 1370 us
  local copies, waits for them, and re-layouts: 94.1 us -> 49.9 us
    all_gather x3 -> x0, waiting for transfers between devices: 215 us -> none  [local(): lax.all_gather(grad_in, 'row', axis=1, tiled=True)]
    ppermute x0 -> x3, waiting for transfers between devices: none -> 184 us  [track_cubes_now(): lax.ppermute(next_value, 'row', tuple(((m, (m - arr_next) % upper) for m...]
    reshape x6 -> x0, local copies, waits for them, and re-layouts: 82.5 us -> none  [regroup(): split = full.reshape(row_count, cols, groups, piece)]
    all_gather x1, waiting for transfers between devices: 1240 us -> 1170 us  [local(): lax.all_gather(own_piece, ('groups', 'col'), axis=1, tiled=True)]
    dynamic_slice x0 -> x3, local copies, waits for them, and re-layouts: none -> 26 us  [track_cubes_now(): return jnp.roll(next_value, piece_now * outcome_arr, axis=1)]
    concatenate x0 -> x3, other arithmetic: none -> 22.2 us  [track_cubes_now(): return jnp.roll(next_value, piece_now * outcome_arr, axis=1)]
where the time goes in v1:
time: 1760 us; the launch traced here: 1750 us
  waiting for transfers between devices  1370 us (78%)
  other arithmetic  127 us (7%)
  matrix products  116 us (7%)
  blocking collectives  57 us (3%)
  local copies, waits for them, and re-layouts  49.9 us (3%)
    all_gather x1, waiting for transfers between devices, local(): lax.all_gather(own_piece, ('groups', 'col'), axis=1, tiled=True)  1170 us
    ppermute x3, waiting for transfers between devices, track_cubes_now(): lax.ppermute(next_value, 'row', tuple(((m, (m - arr_next) % upper) for m...  184 us
    dot_general x3, matrix products, local(): lax.dot_general(regroup(track_cubes_now(grad_in)), full_weight, contract,...  116 us
  transfers between devices with their start and end apart: 6, of which 6 were waited for; matrix products, arithmetic and copies ran while one was open for 3% of the time, Pallas kernels for 0%

profile of v1, /device:TPU:1, one launch (start us, length us, event | category | flops | bytes accessed | tf_op | source)
XLA Modules:
  0.0 1748.6 jit_solution(14925449148972596899)
XLA Ops:
  7.2 7.7 constant_dynamic-slice_fusion
  14.9 2.1 select_bitcast_fusion
  17.0 2.1 collective-permute-start
  19.2 10.1 convert_element_type.29
  29.2 0.6 compare_reduce_fusion.2
  29.8 9.6 bitcast_add_fusion
  39.4 47.6 %collective-permute-done = bf16[384,4096]{1,0:T(8,128)(2,1)} collective-permute-done((bf16[384,4096]{1,0:T(8,128)(2,1)S(1)}, bf16[384,4096]{1,0:T(8,128)(2,1)}, u32[]{:S(2)}, u32[]{:S(2)}) %collective-permute-start) | collective-permute-done | bytes 3145760 | tf_op jit(solution)/shard_map/ppermute | solution.py:19
  87.0 7.4 fusion.13
  94.4 8.7 copy.8
  103.1 6.2 copy.9
  109.3 1174.7 %all-gather.3.cloned.1.call-done = bf16[1,4096,8192]{2,1,0:T(8,128)(2,1)} async-done(((bf16[1,4096,1024]{2,1,0:T(8,128)(2,1)}), bf16[1,4096,8192]{2,1,0:T(8,128)(2,1)}) %all-gather.3.cloned.1.call-update) | async-done | bytes 67108880 | tf_op jit(solution)/shard_map/all_gather | solution.py:55
  1284.0 36.7 %fusion.19 = (f32[384]{0:T(512)S(1)}, f32[384]{0:T(512)S(1)}, f32[384]{0:T(512)S(1)}, f32[384]{0:T(512)S(1)}, f32[384,4096]{1,0:T(8,128)}) fusion(f32[2,384,4096]{2,1,0:T(8,128)} %bitcast_add_fusion, s32[]{:T(128)S(6)} %min.12, f32[1,2,384,4096]{3,2,1,0:T(8,128)} %convert_element_type.29, bf16[384,8192]{0,1:T(8,128)(2,1)} %bitcast.172, ...), kind=kOutput, calls=%fused_computation.36 | convolution fusion | flops 25783959552 | bytes 92297216 | tf_op jit(solution)/shard_map/dot_general | solution.py:75
  1320.8 3.8 all-reduce.2
  1324.6 11.2 multiply_reduce_fusion.2
  1335.8 4.2 psum.120
  1340.0 8.1 fusion.50
  1348.2 5.1 collective-permute-start.1
  1353.3 5.1 collective-permute-done.1
  1358.4 2.3 bitcast_select_fusion
  1360.7 1.3 collective-permute-start.2
  1361.9 68.2 %collective-permute-done.2 = bf16[384,4096]{1,0:T(8,128)(2,1)} collective-permute-done((bf16[384,4096]{1,0:T(8,128)(2,1)S(1)}, bf16[384,4096]{1,0:T(8,128)(2,1)}, u32[]{:S(2)}, u32[]{:S(2)}) %collective-permute-start.2) | collective-permute-done | bytes 3145760 | tf_op jit(solution)/shard_map/ppermute | solution.py:19
  1430.1 7.5 fusion.10
  1437.6 8.6 copy.10
  1446.2 3.4 copy.11
  1449.7 39.6 %fusion.30 = (f32[384]{0:T(512)S(1)}, f32[384]{0:T(512)S(1)}, f32[384]{0:T(512)S(1)}, f32[384]{0:T(512)S(1)}, f32[384,4096]{1,0:T(8,128)}) fusion(f32[2,384,4096]{2,1,0:T(8,128)} %bitcast_add_fusion, s32[]{:T(128)S(6)} %min.11, f32[1,2,384,4096]{3,2,1,0:T(8,128)} %convert_element_type.29, bf16[384,8192]{0,1:T(8,128)(2,1)S(1)} %bitcast.174, ...), kind=kOutput, calls=%fused_computation.54 | convolution fusion | flops 25783959552 | bytes 92297216 | tf_op jit(solution)/shard_map/dot_general | solution.py:75
  1489.3 3.8 all-reduce.1
  1493.1 10.4 multiply_reduce_fusion.1
  1503.6 3.9 psum.123
  1507.5 8.1 fusion.49
  1515.6 1.6 copy-done.3
  1517.2 5.7 collective-permute-start.3
  1522.9 5.1 collective-permute-done.3
  1528.0 1.6 copy-done.4
  1529.6 0.2 broadcast_select_fusion
  1529.9 1.3 collective-permute-start.4
  1531.2 68.1 %collective-permute-done.4 = bf16[384,4096]{1,0:T(8,128)(2,1)} collective-permute-done((bf16[384,4096]{1,0:T(8,128)(2,1)S(1)}, bf16[384,4096]{1,0:T(8,128)(2,1)}, u32[]{:S(2)}, u32[]{:S(2)}) %collective-permute-start.4) | collective-permute-done | bytes 3145760 | tf_op jit(solution)/shard_map/ppermute | solution.py:19
  1599.3 7.4 fusion.7
  1606.7 8.7 copy.12
  1615.4 3.4 copy.13
  1618.8 39.8 %fusion.41 = (f32[384]{0:T(512)S(1)}, f32[384]{0:T(512)S(1)}, f32[384]{0:T(512)S(1)}, f32[384]{0:T(512)S(1)}, f32[384,4096]{1,0:T(8,128)}) fusion(f32[2,384,4096]{2,1,0:T(8,128)} %bitcast_add_fusion, s32[]{:T(128)S(6)} %min.10, f32[1,2,384,4096]{3,2,1,0:T(8,128)} %convert_element_type.29, bf16[384,8192]{0,1:T(8,128)(2,1)S(1)} %bitcast.173, ...), kind=kOutput, calls=%fused_computation.72 | convolution fusion | flops 25783959552 | bytes 92297216 | tf_op jit(solution)/shard_map/dot_general | solution.py:75
  1658.6 3.8 all-reduce
  1662.5 10.5 multiply_reduce_fusion
  1672.9 4.0 psum.126
  1676.9 9.4 fusion.48
  1686.4 14.4 select_reduce_fusion.1
  1700.8 33.4 %psum.127 = f32[4096]{0:T(1024)S(1)} all-reduce(f32[4096]{0:T(1024)S(1)} %add_add_fusion), channel_id=1, replica_groups=mesh['groups'=2,'section'=2,'row'=2,'col'=4] {'section','col'}, use_global_device_ids=true, to_apply=%region_33.35 | all-reduce | flops 4096 | bytes 32768 | tf_op jit(solution)/shard_map/psum | solution.py:112
  1734.2 0.6 broadcast_multiply_fusion
  1734.8 6.7 select_select_fusion
  (45 shorter events, 0.3 us)
Async XLA Ops:
  7.2 1276.9 %all-gather.3.cloned.1.call-start = ((), (), s32[]{:S(2)}) async-start(), calls=%async_computation | async-start | bytes 75497472 | tf_op jit(solution)/shard_map/all_gather | solution.py:55
  14.9 4.2 copy-start.12
  14.9 4.3 copy-start.15
  17.0 70.0 %collective-permute-start = (bf16[384,4096]{1,0:T(8,128)(2,1)S(1)}, bf16[384,4096]{1,0:T(8,128)(2,1)}, u32[]{:S(2)}, u32[]{:S(2)}) collective-permute-start(bf16[384,4096]{1,0:T(8,128)(2,1)S(1)} %select_bitcast_fusion), channel_id=1, source_target_pairs={{0,4},{4,0},{1,5},{5,1},{2,6},{6,2},{3,7},{7,3},{8,12},{12,8},{9,1... | collective-permute-start | bytes 9437192 | tf_op jit(solution)/shard_map/ppermute | solution.py:19
  19.2 10.1 copy-start.16
  1324.6 15.4 copy-start.6
  1324.6 15.4 copy-start.8
  1340.0 8.1 copy-start.10
  1348.2 10.2 copy-start.1
  1348.2 10.2 collective-permute-start.1
  1360.7 69.5 %collective-permute-start.2 = (bf16[384,4096]{1,0:T(8,128)(2,1)S(1)}, bf16[384,4096]{1,0:T(8,128)(2,1)}, u32[]{:S(2)}, u32[]{:S(2)}) collective-permute-start(bf16[384,4096]{1,0:T(8,128)(2,1)S(1)} %bitcast_select_fusion), channel_id=1, source_target_pairs={{0,4},{4,0},{1,5},{5,1},{2,6},{6,2},{3,7},{7,3},{8,12},{12,8},{9,1... | collective-permute-start | bytes 9437192 | tf_op jit(solution)/shard_map/ppermute | solution.py:19
  1449.6 43.5 %copy-start.13 = (pred[384]{0:T(512)(128)(4,1)S(1)}, pred[384]{0:T(512)(128)(4,1)}, u32[]{:S(2)}) copy-start(pred[384]{0:T(512)(128)(4,1)} %get-tuple-element.26) | copy-start | bytes 1156
  1515.6 1.6 copy-start.3
  1517.2 13.9 copy-start.14
  1517.2 10.8 collective-permute-start.3
  1528.0 1.6 copy-start.4
  1529.9 69.5 %collective-permute-start.4 = (bf16[384,4096]{1,0:T(8,128)(2,1)S(1)}, bf16[384,4096]{1,0:T(8,128)(2,1)}, u32[]{:S(2)}, u32[]{:S(2)}) collective-permute-start(bf16[384,4096]{1,0:T(8,128)(2,1)S(1)} %broadcast_select_fusion), channel_id=1, source_target_pairs={{0,4},{4,0},{1,5},{5,1},{2,6},{6,2},{3,7},{7,3},{8,12},{12,8},{9,1... | collective-permute-start | bytes 9437192 | tf_op jit(solution)/shard_map/ppermute | solution.py:19
  1618.8 43.6 %copy-start.5 = (bf16[384,4096]{1,0:T(8,128)(2,1)S(1)}, bf16[384,4096]{1,0:T(8,128)(2,1)}, u32[]{:S(2)}) copy-start(bf16[384,4096]{1,0:T(8,128)(2,1)} %copy-done.4) | copy-start | bytes 9437188
  1676.9 9.4 copy-start
  1676.9 9.4 copy-start.7
  1676.9 9.4 copy-start.9
  1676.9 9.4 copy-start.11
  1686.3 48.4 %copy-start.2 = (bf16[384,4096]{1,0:T(8,128)(2,1)S(1)}, bf16[384,4096]{1,0:T(8,128)(2,1)}, u32[]{:S(2)}) copy-start(bf16[384,4096]{1,0:T(8,128)(2,1)} %copy-done.1) | copy-start | bytes 9437188
Sparse Core Ops, SparseCore 0:
  15.0 1268.9 all-gather.2
